TPU v7x, 32 devices: a whole 2x2x4 slice. The times are simulated.
32 devices in a mesh: dp: 8 (over z, x), tensor: 4 (over y, core).
Axes of the slice: x: 2, y: 2, z: 4, core: 2. Of those that a mesh axis runs over, the one named last changes fastest.
Arguments:
- tokens: bfloat16 [16384, 768], P('dp'), may hold values from -6 to 6
- segments: int32 [16, 1024], P('dp'), may hold values from 0 to 7, never falling along the last dimension, each value on 1 to 512 neighbouring positions
- w_query: bfloat16 [768, 768], P(None, 'tensor'), may hold values from -0.3125 to 0.3125
- b_query: bfloat16 [768], P('tensor'), may hold values from -3 to 3
- w_key: bfloat16 [768, 768], P(None, 'tensor'), may hold values from -0.3125 to 0.3125
- w_value: bfloat16 [768, 768], P(None, 'tensor'), may hold values from -0.21875 to 0.21875
- b_value: bfloat16 [768], P('tensor'), may hold values from -3 to 3
- w_out: bfloat16 [768, 768], P('tensor'), may hold values from -0.875 to 0.875
- b_out: float32 [768], replicated, may hold values from -2 to 2
- gain_one: float32 [768], replicated, may hold values from 0.5 to 1.5
- shift_one: float32 [768], replicated, may hold values from -2 to 2
- w_up: bfloat16 [768, 3072], P(None, 'tensor'), may hold values from -0.21875 to 0.21875
- b_up: float32 [3072], P('tensor'), may hold values from -3 to 3
- w_down: bfloat16 [3072, 768], P('tensor'), may hold values from -0.21875 to 0.21875
- b_down: float32 [768], replicated, may hold values from -2 to 2
- gain_two: float32 [768], replicated, may hold values from 0.5 to 1.5
- shift_two: float32 [768], replicated, may hold values from -2 to 2
- head_gate: float32 [12], P('tensor'), may hold values from 0.2 to 1
- unit_gate: float32 [3072], P('tensor'), may hold values from 0.2 to 1
- hidden_gate: float32 [768], replicated, may hold values from 0.4 to 1
- branch_gate: float32 [2], replicated, may hold values from 0.5 to 1
- cotangent: bfloat16 [16384, 768], P('dp'), may hold values from -6 to 6
Outputs:
- out: bfloat16 [16384, 768], P(('dp', 'tensor'))
- tokens_grad: float32 [16384, 768], P(('dp', 'tensor'))
- w_query_grad: float32 [768, 768], P('dp', 'tensor')
- b_query_grad: float32 [768], P('tensor')
- w_key_grad: float32 [768, 768], P('dp', 'tensor')
- w_value_grad: float32 [768, 768], P('dp', 'tensor')
- b_value_grad: float32 [768], P('tensor')
- w_out_grad: float32 [768, 768], P('tensor', 'dp')
- b_out_grad: float32 [768], replicated
- gain_one_grad: float32 [768], replicated
- shift_one_grad: float32 [768], replicated
- w_up_grad: float32 [768, 3072], P('dp', 'tensor')
- b_up_grad: float32 [3072], P('tensor')
- w_down_grad: float32 [3072, 768], P('tensor', 'dp')
- b_down_grad: float32 [768], replicated
- gain_two_grad: float32 [768], replicated
- shift_two_grad: float32 [768], replicated
- head_gate_grad: float32 [12], P('tensor')
- unit_gate_grad: float32 [3072], P('tensor')
- hidden_gate_grad: float32 [768], replicated
- branch_gate_grad: float32 [2], replicated
Inputs may be any that keep to these rules, and one draw needn't show every extreme that they name: `segments`: within each sequence the numbers never fall; each of the 8 documents has 1 to 512 tokens, one exactly 512.
All inputs are finite; a program needn't handle non-finite values.
Results may differ from a plain program's by a relative error of at most 0.013.
The roundings to bfloat16 on the way count: a program that leaves them out, or rounds other values in their place, can miss the bound.
Values may be sent and summed in bfloat16 or wider, within the bound.
No kernel may reach another device: no remote copies, remote signals or barrier semaphores. Data moves between devices by JAX's collectives and lax.ppermute only.
A program may use at most 128 MiB of HBM per device.

v0:
```python
import jax
import jax.numpy as jnp
from jax import lax
from jax.sharding import PartitionSpec as P

HEAD_DIM = 64
LEN = 1024


def normalize(row_data):
    centre = row_data - jnp.mean(row_data, axis=-1, keepdims=True)
    return centre * lax.rsqrt(jnp.mean(centre * centre, axis=-1, keepdims=True) + 1e-12)


def attention_rows(attn_sum, token_rows, b_out, gain_one, shift_one, hidden_gate, first_gate):
    branch = (attn_sum + b_out) * first_gate * hidden_gate
    return (normalize(token_rows + branch) * gain_one + shift_one) * hidden_gate


def output_rows(down_sum, normed, b_down, gain_two, shift_two, hidden_gate, second_gate):
    branch = (down_sum + b_down) * second_gate * hidden_gate
    return (normalize(normed + branch) * gain_two + shift_two) * hidden_gate


def exact_gelu(inputs):
    return jax.nn.gelu(inputs, approximate=False)


def own_rows(array, pieces):
    row_count = array.shape[0] // pieces
    return lax.dynamic_slice_in_dim(array, lax.axis_index("tensor") * row_count, row_count, 0)


def add_rows(running_sum, update, first_row):
    current = lax.dynamic_slice_in_dim(running_sum, first_row, update.shape[0], 0)
    return lax.dynamic_update_slice_in_dim(running_sum, current + update, first_row, 0)


def block_operands(block_index, queries, key_all, value_all, doc_flat, block_rows, head_count):
    per_seq = LEN // block_rows
    seq_start = block_index // per_seq * LEN
    row_start = block_index * block_rows
    query_rows = lax.dynamic_slice_in_dim(queries, row_start, block_rows, 0).reshape(
        block_rows, head_count, HEAD_DIM
    )
    key_rows = lax.dynamic_slice_in_dim(key_all, seq_start, LEN, 0).reshape(
        LEN, head_count, HEAD_DIM
    )
    value_rows = lax.dynamic_slice_in_dim(value_all, seq_start, LEN, 0).reshape(
        LEN, head_count, HEAD_DIM
    )
    query_ids = lax.dynamic_slice_in_dim(doc_flat, row_start, block_rows, 0)
    key_ids = lax.dynamic_slice_in_dim(doc_flat, seq_start, LEN, 0)
    scores = (
        jnp.einsum("qhd,khd->hqk", query_rows, key_rows, preferred_element_type=jnp.float32) * 0.125
    )
    scores = jnp.where((query_ids[:, None] == key_ids[None, :])[None], scores, -1e30)
    return (seq_start, row_start, query_rows, key_rows, value_rows, scores)


def attend(queries, key_all, value_all, doc_flat, head_count):
    block_rows = min(512, LEN)
    total_rows, row_width = queries.shape

    def one_block(block_index):
        operands = block_operands(
            block_index, queries, key_all, value_all, doc_flat, block_rows, head_count
        )
        scores = operands[5]
        row_peak = jnp.max(scores, axis=-1, keepdims=True)
        exponent = jnp.exp(scores - row_peak)
        row_mass = jnp.sum(exponent, axis=-1, keepdims=True)
        attention = (exponent / row_mass).astype(jnp.bfloat16)
        context = jnp.einsum(
            "hqk,khd->qhd", attention, operands[4], preferred_element_type=jnp.float32
        )
        return (context.reshape(block_rows, row_width), (row_peak + jnp.log(row_mass))[:, :, 0])

    context, log_mass = lax.map(one_block, jnp.arange(total_rows // block_rows, dtype=jnp.int32))
    return (context.reshape(total_rows, row_width), log_mass)


def attend_back(queries, key_all, value_all, doc_flat, head_count, log_mass, context_grad):
    block_rows = min(512, LEN)
    total_rows, row_width = queries.shape

    def one_block(running, inputs):
        key_grad, value_grad = running
        block_index, block_mass = inputs
        seq_start, row_start, query_rows, key_rows, value_rows, scores = block_operands(
            block_index, queries, key_all, value_all, doc_flat, block_rows, head_count
        )
        attention = jnp.exp(scores - block_mass[:, :, None])
        grad_rows = lax.dynamic_slice_in_dim(context_grad, row_start, block_rows, 0).reshape(
            block_rows, head_count, HEAD_DIM
        )
        prob_grad = jnp.einsum(
            "qhd,khd->hqk", grad_rows, value_rows, preferred_element_type=jnp.float32
        )
        centred = prob_grad - jnp.sum(attention * prob_grad, axis=-1, keepdims=True)
        score_grad = (attention * centred).astype(jnp.bfloat16)
        query_step = (
            jnp.einsum("hqk,khd->qhd", score_grad, key_rows, preferred_element_type=jnp.float32)
            * 0.125
        )
        key_step = (
            jnp.einsum("hqk,qhd->khd", score_grad, query_rows, preferred_element_type=jnp.float32)
            * 0.125
        )
        value_step = jnp.einsum(
            "hqk,qhd->khd",
            attention.astype(jnp.bfloat16),
            grad_rows,
            preferred_element_type=jnp.float32,
        )
        key_grad = add_rows(key_grad, key_step.reshape(LEN, row_width), seq_start)
        value_grad = add_rows(value_grad, value_step.reshape(LEN, row_width), seq_start)
        return ((key_grad, value_grad), query_step.reshape(block_rows, row_width))

    blank_grad = jnp.zeros((total_rows, row_width), jnp.float32)
    block_ids = jnp.arange(total_rows // block_rows, dtype=jnp.int32)
    (key_grad, value_grad), query_grad = lax.scan(
        one_block, (blank_grad, blank_grad), (block_ids, log_mass)
    )
    return (query_grad.reshape(total_rows, row_width), key_grad, value_grad)


def local(
    tokens,
    segments,
    w_query,
    b_query,
    w_key,
    w_value,
    b_value,
    w_out,
    b_out,
    gain_one,
    shift_one,
    w_up,
    b_up,
    w_down,
    b_down,
    gain_two,
    shift_two,
    head_gate,
    unit_gate,
    hidden_gate,
    branch_gate,
    cotangent,
):
    pieces = lax.axis_size("tensor")
    head_count = w_query.shape[1] // HEAD_DIM
    doc_flat = segments.reshape(-1)
    token_float = tokens.astype(jnp.float32)
    queries = (
        jnp.dot(tokens, w_query, preferred_element_type=jnp.float32) + b_query.astype(jnp.float32)
    ).astype(jnp.bfloat16)
    key_all = jnp.dot(tokens, w_key, preferred_element_type=jnp.float32).astype(jnp.bfloat16)
    value_all = (
        jnp.dot(tokens, w_value, preferred_element_type=jnp.float32) + b_value.astype(jnp.float32)
    ).astype(jnp.bfloat16)
    context, log_mass = attend(queries, key_all, value_all, doc_flat, head_count)
    column_gate = jnp.repeat(head_gate, HEAD_DIM)
    gated = (context * column_gate[None, :]).astype(jnp.bfloat16)
    attn_part = jnp.dot(gated, w_out, preferred_element_type=jnp.float32)
    attn_total = lax.psum(attn_part, "tensor")
    normed, attn_back = jax.vjp(
        attention_rows,
        attn_total,
        token_float,
        b_out,
        gain_one,
        shift_one,
        hidden_gate,
        branch_gate[0],
    )
    normed_low = normed.astype(jnp.bfloat16)
    up_in = jnp.dot(normed_low, w_up, preferred_element_type=jnp.float32) + b_up
    unit_act, gelu_back = jax.vjp(exact_gelu, up_in)
    unit_out = (unit_act * unit_gate[None, :]).astype(jnp.bfloat16)
    down_part = jnp.dot(unit_out, w_down, preferred_element_type=jnp.float32)
    down_total = lax.psum(down_part, "tensor")
    result, output_back = jax.vjp(
        output_rows, down_total, normed, b_down, gain_two, shift_two, hidden_gate, branch_gate[1]
    )
    down_grad, normed_res, b_down_grad, gain_two_grad, shift_two_grad, hidden_two, second_grad = (
        output_back(cotangent.astype(jnp.float32))
    )
    down_low = down_grad.astype(jnp.bfloat16)
    w_down_grad = jnp.einsum("tu,td->ud", unit_out, down_low, preferred_element_type=jnp.float32)
    unit_grad = jnp.einsum("td,ud->tu", down_low, w_down, preferred_element_type=jnp.float32)
    unit_gate_grad = jnp.sum(unit_grad * unit_act, axis=0)
    up_grad = gelu_back(unit_grad * unit_gate[None, :])[0].astype(jnp.bfloat16)
    b_up_grad = jnp.sum(up_grad.astype(jnp.float32), axis=0)
    w_up_grad = jnp.einsum("td,tu->du", normed_low, up_grad, preferred_element_type=jnp.float32)
    normed_part = jnp.einsum("tu,du->td", up_grad, w_up, preferred_element_type=jnp.float32)
    normed_total = lax.psum(normed_part, "tensor")
    attn_grad, token_res, b_out_grad, gain_one_grad, shift_one_grad, hidden_one, first_grad = (
        attn_back(normed_total + normed_res)
    )
    attn_low = attn_grad.astype(jnp.bfloat16)
    w_out_grad = jnp.einsum("te,td->ed", gated, attn_low, preferred_element_type=jnp.float32)
    gated_grad = jnp.einsum("td,ed->te", attn_low, w_out, preferred_element_type=jnp.float32)
    head_gate_grad = jnp.sum((gated_grad * context).reshape(-1, head_count, HEAD_DIM), axis=(0, 2))
    context_grad = (gated_grad * column_gate[None, :]).astype(jnp.bfloat16)
    query_grad, key_grad, value_grad = attend_back(
        queries, key_all, value_all, doc_flat, head_count, log_mass, context_grad
    )
    query_low = query_grad.astype(jnp.bfloat16)
    key_low = key_grad.astype(jnp.bfloat16)
    value_low = value_grad.astype(jnp.bfloat16)
    b_query_grad = jnp.sum(query_low.astype(jnp.float32), axis=0)
    b_value_grad = jnp.sum(value_low.astype(jnp.float32), axis=0)
    w_query_grad = jnp.einsum("td,te->de", tokens, query_low, preferred_element_type=jnp.float32)
    w_key_grad = jnp.einsum("td,te->de", tokens, key_low, preferred_element_type=jnp.float32)
    w_value_grad = jnp.einsum("td,te->de", tokens, value_low, preferred_element_type=jnp.float32)
    token_part = jnp.einsum("te,de->td", query_low, w_query, preferred_element_type=jnp.float32)
    token_part = token_part + jnp.einsum(
        "te,de->td", key_low, w_key, preferred_element_type=jnp.float32
    )
    token_part = token_part + jnp.einsum(
        "te,de->td", value_low, w_value, preferred_element_type=jnp.float32
    )
    hidden_gate_grad = hidden_one + hidden_two
    branch_gate_grad = jnp.stack([first_grad, second_grad])
    token_total = lax.psum(token_part.astype(jnp.bfloat16), "tensor").astype(jnp.float32)
    tokens_grad = own_rows(token_total + token_res, pieces)
    out_rows = own_rows(result, pieces)
    summed = lax.psum(
        (
            b_query_grad,
            b_value_grad,
            b_up_grad,
            unit_gate_grad,
            head_gate_grad,
            b_out_grad,
            gain_one_grad,
            shift_one_grad,
            b_down_grad,
            gain_two_grad,
            shift_two_grad,
            hidden_gate_grad,
            branch_gate_grad,
        ),
        "dp",
    )
    local_sums = (summed[0], summed[1], summed[2], summed[3], summed[4])
    weight_sums = (
        lax.psum_scatter(w_query_grad, "dp", scatter_dimension=0, tiled=True),
        lax.psum_scatter(w_key_grad, "dp", scatter_dimension=0, tiled=True),
        lax.psum_scatter(w_value_grad, "dp", scatter_dimension=0, tiled=True),
        lax.psum_scatter(w_out_grad, "dp", scatter_dimension=1, tiled=True),
        lax.psum_scatter(w_up_grad, "dp", scatter_dimension=0, tiled=True),
        lax.psum_scatter(w_down_grad, "dp", scatter_dimension=1, tiled=True),
    )
    return (
        out_rows.astype(jnp.bfloat16),
        tokens_grad,
        weight_sums[0],
        local_sums[0],
        weight_sums[1],
        weight_sums[2],
        local_sums[1],
        weight_sums[3],
        summed[5],
        summed[6],
        summed[7],
        weight_sums[4],
        local_sums[2],
        weight_sums[5],
        summed[8],
        summed[9],
        summed[10],
        local_sums[4],
        local_sums[3],
        summed[11],
        summed[12],
    )


def solution(mesh):
    placed = (
        P("dp", None),
        P("dp", None),
        P(None, "tensor"),
        P("tensor"),
        P(None, "tensor"),
        P(None, "tensor"),
        P("tensor"),
        P("tensor", None),
        P(),
        P(),
        P(),
        P(None, "tensor"),
        P("tensor"),
        P("tensor", None),
        P(),
        P(),
        P(),
        P("tensor"),
        P("tensor"),
        P(),
        P(),
        P("dp", None),
    )
    return jax.shard_map(
        local,
        mesh=mesh,
        in_specs=placed,
        out_specs=(
            P(("dp", "tensor"), None),
            P(("dp", "tensor"), None),
            P("dp", "tensor"),
            P("tensor"),
            P("dp", "tensor"),
            P("dp", "tensor"),
            P("tensor"),
            P("tensor", "dp"),
            P(),
            P(),
            P(),
            P("dp", "tensor"),
            P("tensor"),
            P("tensor", "dp"),
            P(),
            P(),
            P(),
            P("tensor"),
            P("tensor"),
            P(),
            P(),
        ),
        check_vma=False,
    )
```

profile of v0, /device:TPU:0, one launch (start us, length us, event | category | flops | bytes accessed | tf_op | source)
XLA Modules:
  0.0 1137.7 jit_solution(777500085040633144)
XLA Ops:
  17.2 92.0 %while.30 = (s32[]{:T(128)}, f32[4,512,192]{1,0,2:T(4,128)}, f32[4,3,512]{2,1,0:T(4,128)}, s32[4]{0:T(128)}, bf16[2048,192]{0,1:T(8,128)(2,1)S(1)}, /*index=5*/s...) while((s32[]{:T(128)}, f32[4,512,192]{1,0,2:T(4,128)}, ...), condition=%wide.region_3.4_spmd, body=%wide.region_0.3_spmd.sunk | while | flops 422050336 | bytes 27529664 | solution.py:79
  31.0 8.6 dynamic_update_slice.41
  54.0 8.6 dynamic_update_slice.41
  77.0 8.6 dynamic_update_slice.41
  100.0 8.6 dynamic_update_slice.41
  119.5 121.2 %all-reduce.6.cloned.1.call-done = f32[2048,768]{1,0:T(8,128)} async-done(((f32[2048,768]{1,0:T(8,128)}), f32[2048,768]{1,0:T(8,128)}) %all-reduce.6.cloned.1.call-update) | async-done | bytes 6291472 | tf_op jit(solution)/shard_map/psum | solution.py:167
  249.9 17.9 %multiply_convert_fusion.1 = (bf16[2048,768]{1,0:T(8,128)(2,1)S(1)}, f32[2048,768]{1,0:T(8,128)}, f32[2048,768]{1,0:T(8,128)}) fusion(f32[768]{0:T(1024)S(1)} %copy-done.43, f32[768]{0:T(1024)S(1)} %copy-done.45, bf16[2048,768]{1,0:T(8,128)(2,1)S(1)} %multiply_convert_fusion.4, bf16[768,768]{1,0:T(8,128)(2,1)S(1)} %copy-done), kind=kOutput, calls=%fused_computation.62 | convolution fusion | flops 2521300992 | bytes 20060160 | tf_op jit(solution)/shard_map/dot_general | solution.py:179
  274.2 119.6 %all-reduce.8.cloned.1.call-done = f32[2048,768]{1,0:T(8,128)} async-done(((f32[2048,768]{1,0:T(8,128)}), f32[2048,768]{1,0:T(8,128)}) %all-reduce.8.cloned.1.call-update) | async-done | bytes 6291472 | tf_op jit(solution)/shard_map/psum | solution.py:183
  393.9 6.7 fusion.41
  402.5 6.0 fusion.17
  411.6 10.5 convert_reduce_fusion
  428.8 119.4 %all-reduce.10.cloned.1.call-done = f32[2048,768]{1,0:T(8,128)} async-done(((f32[2048,768]{1,0:T(8,128)}), f32[2048,768]{1,0:T(8,128)}) %all-reduce.10.cloned.1.call-update) | async-done | bytes 6291472 | tf_op jit(solution)/shard_map/psum | solution.py:198
  548.2 12.7 %multiply_reduce_fusion.5 = (f32[768]{0:T(1024)}, f32[768]{0:T(1024)}, f32[2048]{0:T(1024)S(1)}, f32[768]{0:T(1024)}, f32[768]{0:T(1024)}, /*index=5*/f32[768]{0:T(1024)}, f32[]{:T(128)}, f32[2048,768]{1,0:T(8,128)S(1)}) fusion(f32[2048,768]{1,0:T(8,128)} %copy-done.2, f32[768]{0:T(1024)S(1)} %copy-done.26, f32[768]{0:T(1024)S(1)} %copy-done.24, ...), kind=kLoop, calls=%fused_computation.52 | loop fusion | flops 37742848 | bytes 31517704 | tf_op jit(solution)/shard_map/transpose(jvp())/reduce_sum | solution.py:17
  565.4 6.7 multiply_reduce_fusion.2
  580.3 74.7 %while.31 = (s32[]{:T(128)}, f32[2048,192]{0,1:T(8,128)}, f32[2048,192]{0,1:T(8,128)S(1)}, bf16[4,512,192]{1,2,0:T(8,128)(2,1)}, s32[4]{0:T(128)S(1)}, /*index=5...) while((s32[]{:T(128)}, f32[2048,192]{0,1:T(8,128)}, ...), condition=%wide.region_17.18_spmd, body=%wide.region_15.17_spmd.sunk | while | flops 1031535104 | bytes 76280352 | solution.py:122
  676.2 7.0 fusion.49
  683.3 8.9 fusion.37
  698.9 38.8 %all-reduce = (f32[192]{0:T(256)}, f32[192]{0:T(256)}, f32[768]{0:T(1024)}, f32[768]{0:T(1024)}, f32[768]{0:T(1024)}, /*index=5*/f32[768]{0:T(1024)}, f32[768]{0...) all-reduce(f32[192]{0:T(256)S(1)} %convert_reduce_fusion.2, ...), channel_id=1, replica_groups=mesh['dp'=8,'tensor'=4] {'dp'}, use_global_device_ids=true, to_apply=%region_21.22 | all-reduce | flops 7301 | bytes 58408 | tf_op jit(solution)/shard_map/psum | solution.py:230
  739.3 49.7 %all-reduce.12.cloned.1.call-done = bf16[2048,768]{1,0:T(8,128)(2,1)} async-done(((bf16[2048,768]{1,0:T(8,128)(2,1)}), bf16[2048,768]{1,0:T(8,128)(2,1)}) %all-reduce.12.cloned.1.call-update) | async-done | bytes 3145744 | tf_op jit(solution)/shard_map/psum | solution.py:227
  791.9 63.7 %reduce-scatter.19.cloned.1.call-done = f32[96,192]{1,0:T(8,128)} async-done(((f32[768,192]{1,0:T(8,128)}), f32[96,192]{1,0:T(8,128)}) %reduce-scatter.19.cloned.1.call-update) | async-done | bytes 73744
  855.6 65.4 %reduce-scatter.21.cloned.1.call-done = f32[96,192]{1,0:T(8,128)} async-done(((f32[768,192]{1,0:T(8,128)}), f32[96,192]{1,0:T(8,128)}) %reduce-scatter.21.cloned.1.call-update) | async-done | bytes 73744
  921.0 65.6 %reduce-scatter.23.cloned.1.call-done = f32[96,192]{1,0:T(8,128)} async-done(((f32[768,192]{1,0:T(8,128)}), f32[96,192]{1,0:T(8,128)}) %reduce-scatter.23.cloned.1.call-update) | async-done | bytes 73744
  986.6 72.1 %reduce-scatter.15.cloned.1.call-done = f32[96,768]{1,0:T(8,128)} async-done(((f32[768,768]{1,0:T(8,128)}), f32[96,768]{1,0:T(8,128)}) %reduce-scatter.15.cloned.1.call-update) | async-done | bytes 294928 | tf_op jit(solution)/shard_map/reduce_scatter | solution.py:254
  1058.7 71.9 %reduce-scatter.17.cloned.1.call-done = f32[768,96]{0,1:T(8,128)} async-done(((f32[768,768]{0,1:T(8,128)}), f32[768,96]{0,1:T(8,128)}) %reduce-scatter.17.cloned.1.call-update) | async-done | bytes 294928 | tf_op jit(solution)/shard_map/reduce_scatter | solution.py:255
  (315 shorter events, 197.8 us)
Async XLA Ops:
  7.2 242.6 %copy-start = (bf16[768,768]{1,0:T(8,128)(2,1)S(1)}, bf16[768,768]{1,0:T(8,128)(2,1)}, u32[]{:S(2)}) copy-start(bf16[768,768]{1,0:T(8,128)(2,1)} %param.37) | copy-start | bytes 3538948
  7.2 233.5 %all-reduce.6.cloned.1.call-start = ((), (), s32[]{:S(2)}) async-start(), calls=%async_computation.6 | async-start | bytes 12582912 | tf_op jit(solution)/shard_map/psum | solution.py:167
  118.3 122.5 %copy-start.15 = (f32[768]{0:T(1024)S(1)}, f32[768]{0:T(1024)}, u32[]{:S(2)}) copy-start(f32[768]{0:T(1024)} %param.45) | copy-start | bytes 9220
  118.3 122.5 %copy-start.37 = (f32[768]{0:T(1024)S(1)}, f32[768]{0:T(1024)}, u32[]{:S(2)}) copy-start(f32[768]{0:T(1024)} %param.34) | copy-start | bytes 9220
  118.3 275.6 %all-reduce.8.cloned.1.call-start = ((), (), s32[]{:S(2)}) async-start(), calls=%async_computation.7 | async-start | bytes 12582912 | tf_op jit(solution)/shard_map/psum | solution.py:183
  248.4 19.4 %copy-start.20 = (f32[2048]{0:T(1024)}, f32[2048]{0:T(1024)S(1)}, u32[]{:S(2)}) copy-start(f32[2048]{0:T(1024)S(1)} %fusion.32) | copy-start | bytes 24580
  249.8 18.0 %copy-start.12 = (bf16[2048,768]{1,0:T(8,128)(2,1)}, bf16[2048,768]{1,0:T(8,128)(2,1)S(1)}, u32[]{:S(2)}) copy-start(bf16[2048,768]{1,0:T(8,128)(2,1)S(1)} %multiply_convert_fusion.4) | copy-start | bytes 9437188
  249.8 19.6 %copy-start.41 = (bf16[768,768]{1,0:T(8,128)(2,1)S(1)}, bf16[768,768]{1,0:T(8,128)(2,1)}, u32[]{:S(2)}) copy-start(bf16[768,768]{1,0:T(8,128)(2,1)} %param.39) | copy-start | bytes 3538948
  273.9 274.3 %all-reduce.10.cloned.1.call-start = ((), (), s32[]{:S(2)}) async-start(), calls=%async_computation.8 | async-start | bytes 12582912 | tf_op jit(solution)/shard_map/psum | solution.py:198
  411.5 10.6 copy-start.7
  428.3 120.0 %copy-start.21 = (f32[2048]{0:T(1024)S(1)}, f32[2048]{0:T(1024)}, u32[]{:S(2)}) copy-start(f32[2048]{0:T(1024)} %copy-done.20) | copy-start | bytes 24580
  428.3 120.0 %copy-start.26 = (f32[768]{0:T(1024)S(1)}, f32[768]{0:T(1024)}, u32[]{:S(2)}) copy-start(f32[768]{0:T(1024)} %param.36) | copy-start | bytes 9220
  428.3 120.0 %copy-start.28 = (f32[2048]{0:T(1024)S(1)}, f32[2048]{0:T(1024)}, u32[]{:S(2)}) copy-start(f32[2048]{0:T(1024)} %copy-done.27) | copy-start | bytes 24580
  428.3 120.0 %copy-start.33 = (f32[768]{0:T(1024)S(1)}, f32[768]{0:T(1024)}, u32[]{:S(2)}) copy-start(f32[768]{0:T(1024)} %param.40) | copy-start | bytes 9220
  428.3 309.4 %reduce-scatter.25.cloned.1.call-start = ((), (), s32[]{:S(2)}) async-start(), calls=%async_computation.15 | async-start | bytes 884736
  428.8 132.1 %copy-start.23 = (f32[2048]{0:T(1024)S(1)}, f32[2048]{0:T(1024)}, u32[]{:S(2)}) copy-start(f32[2048]{0:T(1024)} %copy-done.22) | copy-start | bytes 24580
  656.3 132.7 %all-reduce.12.cloned.1.call-start = ((), (), s32[]{:S(2)}) async-start(), calls=%async_computation.9 | async-start | bytes 6291456 | tf_op jit(solution)/shard_map/psum | solution.py:227
  663.7 191.9 %reduce-scatter.19.cloned.1.call-start = ((), (), s32[]{:S(2)}) async-start(), calls=%async_computation.12 | async-start | bytes 884736
  667.6 253.4 %reduce-scatter.21.cloned.1.call-start = ((), (), s32[]{:S(2)}) async-start(), calls=%async_computation.13 | async-start | bytes 884736
  672.2 314.4 %reduce-scatter.23.cloned.1.call-start = ((), (), s32[]{:S(2)}) async-start(), calls=%async_computation.14 | async-start | bytes 884736
  676.2 382.6 %reduce-scatter.15.cloned.1.call-start = ((), (), s32[]{:S(2)}) async-start(), calls=%async_computation.10 | async-start | bytes 2654208 | tf_op jit(solution)/shard_map/reduce_scatter | solution.py:254
  683.3 14.6 %copy-start.13 = (bf16[4,512,192]{1,2,0:T(8,128)(2,1)S(1)}, bf16[4,512,192]{1,2,0:T(8,128)(2,1)}, u32[]{:S(2)}) copy-start(bf16[4,512,192]{1,2,0:T(8,128)(2,1)} %get-tuple-element.266) | copy-start | bytes 2359300
  683.3 447.4 %reduce-scatter.17.cloned.1.call-start = ((), (), s32[]{:S(2)}) async-start(), calls=%async_computation.11 | async-start | bytes 2654208 | tf_op jit(solution)/shard_map/reduce_scatter | solution.py:255
  683.3 447.3 %copy-start.1 = (bf16[768,768]{1,0:T(8,128)(2,1)S(1)}, bf16[768,768]{1,0:T(8,128)(2,1)}, u32[]{:S(2)}) copy-start(bf16[768,768]{1,0:T(8,128)(2,1)} %param.37) | copy-start | bytes 3538948
  (49 other events, 172.9 us)
Sparse Core Ops, SparseCore 0:
  118.4 122.2 all-reduce.5
  274.1 119.7 all-reduce.7
  428.4 119.7 all-reduce.9
  656.4 62.7 reduce-scatter.24
  721.5 67.4 all-reduce.11
  793.1 62.4 reduce-scatter.18
  859.5 61.4 reduce-scatter.20
  925.3 61.3 reduce-scatter.22
  990.7 67.9 reduce-scatter.14
  1062.7 67.9 reduce-scatter.16
where the time goes:
time: 1150 us; the launch traced here: 1140 us
  waiting for transfers between devices  749 us (65%)
  matrix products  130 us (11%)
  local copies, waits for them, and re-layouts  97.1 us (8%)
  other arithmetic  79.7 us (7%)
  blocking collectives  38.8 us (3%)
  loops' own time  26.8 us (2%)
  between operations  15 us (1%)
    unnamed x14, waiting for transfers between devices  195 us
    psum x1, waiting for transfers between devices, local(): attn_total = lax.psum(attn_part, 'tensor')  121 us
    psum x1, waiting for transfers between devices, local(): down_total = lax.psum(down_part, 'tensor')  120 us
    psum x1, waiting for transfers between devices, local(): normed_total = lax.psum(normed_part, 'tensor')  119 us
    reduce_scatter x1, waiting for transfers between devices, local(): lax.psum_scatter(w_up_grad, 'dp', scatter_dimension=0, tiled=True)  72.1 us
    reduce_scatter x1, waiting for transfers between devices, local(): lax.psum_scatter(w_down_grad, 'dp', scatter_dimension=1, tiled=True)  71.9 us
    psum x1, waiting for transfers between devices, local(): lax.psum(token_part.astype(jnp.bfloat16), 'tensor').astype(jnp.float32)  49.7 us
    dynamic_update_slice x12, local copies, waits for them, and re-layouts, attend(): lax.map(one_block, jnp.arange(total_rows // block_rows, dtype=jnp.int32))  38.8 us
  transfers between devices with their start and end apart: 10, of which 9 were waited for; matrix products, arithmetic and copies ran while one was open for 4% of the time, Pallas kernels for 0%

commit v1 on v0

v1 whole, which is shorter than its diff:
```python
import jax
import jax.numpy as jnp
from jax import lax
from jax.sharding import PartitionSpec as P

HEAD_DIM = 64
LEN = 1024
WIDTH = 768
F32 = jnp.float32
BF16 = jnp.bfloat16


def normalize(row_data):
    centre = row_data - jnp.mean(row_data, axis=-1, keepdims=True)
    return centre * lax.rsqrt(jnp.mean(centre * centre, axis=-1, keepdims=True) + 1e-12)


def attention_rows(attn_sum, token_rows, b_out, gain_one, shift_one, hidden_gate, first_gate):
    branch = (attn_sum + b_out) * first_gate * hidden_gate
    return (normalize(token_rows + branch) * gain_one + shift_one) * hidden_gate


def output_rows(down_sum, normed, b_down, gain_two, shift_two, hidden_gate, second_gate):
    branch = (down_sum + b_down) * second_gate * hidden_gate
    return (normalize(normed + branch) * gain_two + shift_two) * hidden_gate


def exact_gelu(inputs):
    return jax.nn.gelu(inputs, approximate=False)


def swap(array, axis, bit):
    size = lax.axis_size(axis)
    return lax.ppermute(array, axis, [(i, i ^ bit) for i in range(size)])


def dot(left, right, left_dim, right_dim):
    return lax.dot_general(
        left, right, (((left_dim,), (right_dim,)), ((), ())), preferred_element_type=F32
    )


def attend(queries, keys, values, same_doc):
    heads = queries.shape[1] // HEAD_DIM
    split = lambda a: a.reshape(LEN, heads, HEAD_DIM)
    scores = jnp.einsum("qhd,khd->hqk", split(queries), split(keys), preferred_element_type=F32) * 0.125
    scores = jnp.where(same_doc[None], scores, -1e30)
    peak = jnp.max(scores, axis=-1, keepdims=True)
    exponent = jnp.exp(scores - peak)
    mass = jnp.sum(exponent, axis=-1, keepdims=True)
    attention = (exponent / mass).astype(BF16)
    context = jnp.einsum("hqk,khd->qhd", attention, split(values), preferred_element_type=F32)
    return context.reshape(LEN, heads * HEAD_DIM), peak + jnp.log(mass)


def attend_back(queries, keys, values, same_doc, log_mass, context_grad):
    heads = queries.shape[1] // HEAD_DIM
    split = lambda a: a.reshape(LEN, heads, HEAD_DIM)
    join = lambda a: a.reshape(LEN, heads * HEAD_DIM).astype(BF16)
    q, k, v, g = split(queries), split(keys), split(values), split(context_grad)
    scores = jnp.einsum("qhd,khd->hqk", q, k, preferred_element_type=F32) * 0.125
    scores = jnp.where(same_doc[None], scores, -1e30)
    attention = jnp.exp(scores - log_mass)
    prob_grad = jnp.einsum("qhd,khd->hqk", g, v, preferred_element_type=F32)
    centred = prob_grad - jnp.sum(attention * prob_grad, axis=-1, keepdims=True)
    score_grad = (attention * centred).astype(BF16)
    query_grad = jnp.einsum("hqk,khd->qhd", score_grad, k, preferred_element_type=F32) * 0.125
    key_grad = jnp.einsum("hqk,qhd->khd", score_grad, q, preferred_element_type=F32) * 0.125
    value_grad = jnp.einsum("hqk,qhd->khd", attention.astype(BF16), g, preferred_element_type=F32)
    return join(query_grad), join(key_grad), join(value_grad)


def fold(grad, axis, bit, rank_bit):
    kept = jnp.where(rank_bit == 0, grad[0], grad[1])
    sent = jnp.where(rank_bit == 0, grad[1], grad[0])
    received = swap(sent.astype(BF16), axis, bit)
    return kept.astype(F32) + received.astype(F32)


def fold_rows(grad, dp_rank, dp_size, first=0):
    bit = 1 << first
    while bit < dp_size:
        blocks, rows, cols = grad.shape
        pairs = grad.reshape(blocks // 2, 2, rows, cols).swapaxes(0, 1)
        grad = fold(pairs, "dp", bit, (dp_rank // bit) % 2)
        bit *= 2
    return grad[0]


def local(
    tokens, segments, w_query, b_query, w_key, w_value, b_value, w_out, b_out, gain_one, shift_one,
    w_up, b_up, w_down, b_down, gain_two, shift_two, head_gate, unit_gate, hidden_gate, branch_gate, cotangent,
):
    rank = lax.axis_index("tensor")
    core, seq = rank % 2, rank // 2
    dp_rank, dp_size = lax.axis_index("dp"), lax.axis_size("dp")
    half = LEN // 2
    attn_own = jnp.concatenate([w_query.T, w_key.T, w_value.T, w_out], axis=0)
    pad = jnp.zeros((WIDTH - 387,), F32)
    small_own = jnp.stack(
        [jnp.concatenate([b_query.astype(F32), b_value.astype(F32), head_gate, pad]), b_up, unit_gate]
    )
    attn_far = swap(attn_own, "tensor", 2)
    small_far = swap(small_own, "tensor", 2)
    mlp_own = jnp.stack([w_up, w_down])
    mlp_far = swap(mlp_own, "tensor", 2)
    mlp_core = swap(mlp_own, "tensor", 1)
    mlp_far_core = swap(mlp_far, "tensor", 1)
    small_core = swap(jnp.stack([small_own, small_far]), "tensor", 1)
    seq_tokens = lax.dynamic_slice_in_dim(tokens, seq * LEN, LEN, 0)
    doc_ids = lax.dynamic_slice_in_dim(segments, seq, 1, 0)[0]
    same_doc = doc_ids[:, None] == doc_ids[None, :]
    attn_pieces = []
    attn_part = 0.0
    for weights, small in ((attn_own, small_own), (attn_far, small_far)):
        both = dot(seq_tokens, weights[:576], 1, 1)
        bias_q, bias_v, gates = small[0, :192], small[0, 192:384], small[0, 384:387]
        queries = (both[:, :192] + bias_q).astype(BF16)
        keys = both[:, 192:384].astype(BF16)
        values = (both[:, 384:576] + bias_v).astype(BF16)
        context, log_mass = attend(queries, keys, values, same_doc)
        column_gate = jnp.repeat(gates, HEAD_DIM)
        gated = (context * column_gate[None, :]).astype(BF16)
        attn_part = attn_part + dot(gated, weights[576:], 1, 0)
        attn_pieces.append((weights, queries, keys, values, context, log_mass, column_gate, gated))
    own_half = lambda a, which: lax.dynamic_slice_in_dim(a, which * half, half, 0)
    attn_total = own_half(attn_part, core) + swap(own_half(attn_part, 1 - core), "tensor", 1)
    row_tokens = own_half(seq_tokens, core)
    row_cotangent = lax.dynamic_slice_in_dim(cotangent, rank * half, half, 0).astype(F32)
    normed, attn_back = jax.vjp(
        attention_rows, attn_total, row_tokens.astype(F32), b_out, gain_one, shift_one, hidden_gate, branch_gate[0]
    )
    normed_low = normed.astype(BF16)
    mlp = [mlp_own, mlp_core, mlp_far, mlp_far_core]
    units = [small_own, small_core[0], small_far, small_core[1]]
    down_total = 0.0
    saved = []
    for weights, small in zip(mlp, units):
        up_in = dot(normed_low, weights[0], 1, 0) + small[1]
        unit_act, gelu_back = jax.vjp(exact_gelu, up_in)
        unit_out = (unit_act * small[2][None, :]).astype(BF16)
        down_total = down_total + dot(unit_out, weights[1], 1, 0)
        saved.append((unit_act, gelu_back, unit_out))
    result, output_back = jax.vjp(
        output_rows, down_total, normed, b_down, gain_two, shift_two, hidden_gate, branch_gate[1]
    )
    down_grad, normed_res, b_down_grad, gain_two_grad, shift_two_grad, hidden_two, second_grad = output_back(
        row_cotangent
    )
    down_low = down_grad.astype(BF16)
    normed_total = normed_res
    mlp_grads, vec_grads = [], []
    for weights, small, (unit_act, gelu_back, unit_out) in zip(mlp, units, saved):
        w_down_t = dot(down_low, unit_out, 0, 0)
        unit_grad = dot(down_low, weights[1], 1, 1)
        gate_grad = jnp.sum(unit_grad * unit_act, axis=0)
        up_grad = gelu_back(unit_grad * small[2][None, :])[0].astype(BF16)
        b_up_part = jnp.sum(up_grad.astype(F32), axis=0)
        w_up_part = dot(normed_low, up_grad, 0, 0)
        normed_total = normed_total + dot(up_grad, weights[0], 1, 1)
        mlp_grads.append(jnp.concatenate([w_up_part, w_down_t], axis=1))
        vec_grads.append(jnp.stack([b_up_part, gate_grad]))
    attn_grad, token_res, b_out_grad, gain_one_grad, shift_one_grad, hidden_one, first_grad = attn_back(normed_total)
    attn_low = attn_grad.astype(BF16)
    other_low = swap(attn_low, "tensor", 1)
    attn_rows = jnp.where(
        core == 0, jnp.concatenate([attn_low, other_low]), jnp.concatenate([other_low, attn_low])
    )
    received = swap(jnp.stack([mlp_grads[1], mlp_grads[3]]).astype(BF16), "tensor", 1).astype(F32)
    near, far = mlp_grads[0] + received[0], mlp_grads[2] + received[1]
    mlp_sum = near + swap(far.astype(BF16), "tensor", 2).astype(F32)
    mlp_block = fold_rows(mlp_sum.reshape(dp_size, WIDTH // dp_size, 2 * WIDTH), dp_rank, dp_size)
    token_part = 0.0
    attn_grads, head_vecs = [], []
    for weights, queries, keys, values, context, log_mass, column_gate, gated in attn_pieces:
        w_out_t = dot(attn_rows, gated, 0, 0)
        gated_grad = dot(attn_rows, weights[576:], 1, 1)
        head_grad = jnp.sum((gated_grad * context).reshape(-1, 3, HEAD_DIM), axis=(0, 2))
        context_grad = (gated_grad * column_gate[None, :]).astype(BF16)
        grads = jnp.concatenate(
            attend_back(queries, keys, values, same_doc, log_mass, context_grad), axis=1
        )
        sums = jnp.sum(grads.astype(F32), axis=0)
        head_vecs.append(jnp.concatenate([sums[:192], sums[384:], head_grad, pad]))
        attn_grads.append(jnp.concatenate([dot(seq_tokens, grads, 0, 0), w_out_t], axis=1))
        token_part = token_part + dot(grads, weights[:576], 1, 0)
    token_total = own_half(token_part, core) + swap(own_half(token_part, 1 - core), "tensor", 1)
    tokens_grad = token_total + token_res
    attn_sum = attn_grads[0] + swap(attn_grads[1].astype(BF16), "tensor", 2).astype(F32)
    attn_block = fold_rows(attn_sum.reshape(dp_size, WIDTH // dp_size, WIDTH), dp_rank, dp_size)
    zero = jnp.zeros((WIDTH,), F32)
    branch_row = jnp.concatenate([jnp.stack([first_grad, second_grad]), jnp.zeros((WIDTH - 2,), F32)])
    common = jnp.stack(
        [b_out_grad, gain_one_grad, shift_one_grad, b_down_grad, gain_two_grad, shift_two_grad,
         hidden_one + hidden_two, branch_row]
    )
    quarter_rows = jnp.zeros((4, 3, WIDTH), F32)
    for index, (flip, heads) in enumerate(((0, head_vecs[0]), (1, None), (2, head_vecs[1]), (3, None))):
        block = jnp.concatenate([(zero if heads is None else heads)[None], vec_grads[index]])
        quarter_rows = lax.dynamic_update_slice(quarter_rows, block[None], (rank ^ flip, 0, 0))
    vectors = jnp.concatenate([common, quarter_rows.reshape(12, WIDTH)])
    vectors = vectors + swap(vectors, "tensor", 1)
    vectors = vectors + swap(vectors, "tensor", 2)
    bit = 1
    while bit < dp_size:
        vectors = vectors + swap(vectors, "dp", bit)
        bit *= 2
    mine = lax.dynamic_slice(vectors, (8 + 3 * rank, 0), (3, WIDTH))
    return (
        result.astype(BF16),
        tokens_grad,
        attn_block[:, :192],
        mine[0, :192],
        attn_block[:, 192:384],
        attn_block[:, 384:576],
        mine[0, 192:384],
        attn_block[:, 576:].T,
        vectors[0],
        vectors[1],
        vectors[2],
        mlp_block[:, :WIDTH],
        mine[1],
        mlp_block[:, WIDTH:].T,
        vectors[3],
        vectors[4],
        vectors[5],
        mine[0, 384:387],
        mine[2],
        vectors[6],
        vectors[7, :2],
    )


def solution(mesh):
    row, col = P("dp", None), P(None, "tensor")
    placed = (
        row, row, col, P("tensor"), col, col, P("tensor"), P("tensor", None), P(), P(), P(), col, P("tensor"),
        P("tensor", None), P(), P(), P(), P("tensor"), P("tensor"), P(), P(), row,
    )
    rows, part, turned = P(("dp", "tensor"), None), P("dp", "tensor"), P("tensor", "dp")
    return jax.shard_map(
        local,
        mesh=mesh,
        in_specs=placed,
        out_specs=(
            rows, rows, part, P("tensor"), part, part, P("tensor"), turned, P(), P(), P(), part, P("tensor"),
            turned, P(), P(), P(), P("tensor"), P("tensor"), P(), P(),
        ),
        check_vma=False,
    )
```

time: 1150 us -> 403 us (0.35)
  waiting for transfers between devices: 749 us -> 111 us
  local copies, waits for them, and re-layouts: 97.1 us -> 48.9 us
  blocking collectives: 38.8 us -> 0 us
  loops' own time: 26.8 us -> 0 us
  starting transfers between devices: 1.56 us -> 20.9 us
  between operations: 15 us -> 2.39 us
  matrix products: 130 us -> 142 us
    psum x4 -> x0, waiting for transfers between devices: 410 us -> none  [the longest x1 121 us: local(): attn_total = lax.psum(attn_part, 'tensor')]
    unnamed x14 -> x0, waiting for transfers between devices: 195 us -> none
    reduce_scatter x2 -> x0, waiting for transfers between devices: 144 us -> none  [the longest x1 72.1 us: local(): lax.psum_scatter(w_up_grad, 'dp', scatter_dimension=0, tiled=True)]
    ppermute x0 -> x23, waiting for transfers between devices: none -> 111 us  [swap(): return lax.ppermute(array, axis, [(i, i ^ bit) for i in range(size)])]
    dynamic_update_slice x12 -> x0, local copies, waits for them, and re-layouts: 38.8 us -> none  [attend(): lax.map(one_block, jnp.arange(total_rows // block_rows, dtype=jnp.int32))]
    psum x1 -> x0, blocking collectives: 38.8 us -> none  [local(): lax.psum((b_query_grad, b_value_grad, b_up_grad, unit_gate_grad, head_gat...]
    dynamic_slice x48 -> x3, local copies, waits for them, and re-layouts: 33.8 us -> 1.36 us  [the longest x2 1.36 us: local(): lax.dynamic_slice_in_dim(a, which * half, half, 0)]
    another operation x2 -> x0, loops' own time: 26.8 us -> none  [the longest x1 13.6 us: attend_back(): lax.scan(one_block, (blank_grad, blank_grad), (block_ids, log_mass))]
  transfers between devices with their start and end apart: 10 -> 23, of which waited for: 9 -> 10; matrix products, arithmetic and copies ran while one was open for 4% -> 51% of each run, Pallas kernels for 0% -> 0%
where the time goes in v1:
time: 403 us; the launch traced here: 399 us
  matrix products  142 us (35%)
  waiting for transfers between devices  111 us (28%)
  other arithmetic  74.2 us (18%)
  local copies, waits for them, and re-layouts  48.9 us (12%)
  starting transfers between devices  20.9 us (5%)
    ppermute x23, waiting for transfers between devices, swap(): return lax.ppermute(array, axis, [(i, i ^ bit) for i in range(size)])  111 us
    dot_general x36, matrix products, dot(): lax.dot_general(left, right, (((left_dim,), (right_dim,)), ((), ())), pre...  102 us
    ppermute x23, starting transfers between devices, swap(): return lax.ppermute(array, axis, [(i, i ^ bit) for i in range(size)])  20.9 us
    unnamed x191, local copies, waits for them, and re-layouts  15.6 us
    dot_general x2, matrix products, attend_back(): prob_grad = jnp.einsum('qhd,khd->hqk', g, v, preferred_element_type=F32)  11.4 us
    convert_element_type x2, other arithmetic, attend_back(): score_grad = (attention * centred).astype(BF16)  10.9 us
    dot_general x2, matrix products, attend_back(): jnp.einsum('hqk,qhd->khd', score_grad, q, preferred_element_type=F32)  10 us
  transfers between devices with their start and end apart: 23, of which 10 were waited for; matrix products, arithmetic and copies ran while one was open for 51% of the time, Pallas kernels for 0%

profile of v1, /device:TPU:0, one launch (start us, length us, event | category | flops | bytes accessed | tf_op | source)
XLA Modules:
  0.0 399.3 jit_solution(17198186743517232626)
XLA Ops:
  19.3 3.4 fusion.121
  33.7 4.5 %collective-permute-done = bf16[768,768]{1,0:T(8,128)(2,1)} collective-permute-done((bf16[768,768]{1,0:T(8,128)(2,1)S(1)}, bf16[768,768]{1,0:T(8,128)(2,1)}, u32[]{:S(2)}, u32[]{:S(2)}) %collective-permute-start) | collective-permute-done | bytes 1179680 | tf_op jit(solution)/shard_map/ppermute | solution.py:34
  41.2 3.2 fusion.122
  64.1 23.2 %collective-permute-done.5 = bf16[2,768,768]{2,1,0:T(8,128)(2,1)} collective-permute-done((bf16[2,768,768]{2,1,0:T(8,128)(2,1)}, bf16[2,768,768]{2,1,0:T(8,128)(2,1)}, u32[]{:S(2)}, u32[]{:S(2)}) %collective-permute-start.5) | collective-permute-done | bytes 2359328 | tf_op jit(solution)/shard_map/ppermute | solution.py:34
  91.4 11.2 %multiply_convert_fusion.4 = (bf16[512,768]{1,0:T(8,128)(2,1)S(1)}, f32[512,768]{1,0:T(8,128)S(1)}, f32[512,768]{1,0:T(8,128)S(1)}) fusion(f32[768]{0:T(1024)S(1)} %get-tuple-element.112, f32[768]{0:T(1024)S(1)} %get-tuple-element.111, bf16[512,768]{1,0:T(8,128)(2,1)S(1)} %multiply_convert_fusion.9, bf16[2,768,768]{2,1,0:T(8,128)(2,1)} %collective-permute-done.5), kind=kOutput, calls=%fused_computation.100 | convolution fusion | flops 630325248 | bytes 5904384 | tf_op jit(solution)/shard_map/dot_general | solution.py:38
  102.7 9.9 %multiply_convert_fusion.6 = (bf16[512,768]{1,0:T(8,128)(2,1)S(1)}, f32[512,768]{1,0:T(8,128)S(1)}, f32[512,768]{1,0:T(8,128)S(1)}) fusion(f32[768]{0:T(1024)S(1)} %copy-done.76, f32[768]{0:T(1024)S(1)} %copy-done.75, bf16[512,768]{1,0:T(8,128)(2,1)S(1)} %multiply_convert_fusion.9, bf16[768,768]{1,0:T(8,128)(2,1)S(1)} %copy-done.36), kind=kOutput, calls=%fused_computation.126 | convolution fusion | flops 630325248 | bytes 5904384 | tf_op jit(solution)/shard_map/dot_general | solution.py:38
  115.5 10.9 %multiply_convert_fusion.5 = (bf16[512,768]{1,0:T(8,128)(2,1)S(1)}, f32[512,768]{1,0:T(8,128)S(1)}, f32[512,768]{1,0:T(8,128)S(1)}) fusion(f32[768]{0:T(1024)S(1)} %get-tuple-element.109, f32[768]{0:T(1024)S(1)} %get-tuple-element.110, bf16[512,768]{1,0:T(8,128)(2,1)S(1)} %multiply_convert_fusion.9, bf16[2,768,768]{2,1,0:T(8,128)(2,1)} %collective-permute-done.3), kind=kOutput, calls=%fused_computation.113 | convolution fusion | flops 630325248 | bytes 5904384 | tf_op jit(solution)/shard_map/dot_general | solution.py:38
  128.5 10.3 %multiply_convert_fusion.3 = (bf16[512,768]{1,0:T(8,128)(2,1)S(1)}, f32[512,768]{1,0:T(8,128)S(1)}, f32[512,768]{1,0:T(8,128)S(1)}) fusion(f32[768]{0:T(1024)S(1)} %get-tuple-element.108, f32[768]{0:T(1024)S(1)} %get-tuple-element.107, bf16[512,768]{1,0:T(8,128)(2,1)S(1)} %multiply_convert_fusion.9, bf16[2,768,768]{2,1,0:T(8,128)(2,1)S(1)} %collective-permute-done.6), kind=kOutput, calls=%fused_computation.87 | convolution fusion | flops 630325248 | bytes 5906432 | tf_op jit(solution)/shard_map/dot_general | solution.py:38
  166.0 3.4 multiply_reduce_fusion.10
  195.0 3.7 multiply_reduce_fusion
  198.7 5.3 %multiply_convert_fusion = bf16[3,1024,1024]{1,2,0:T(8,128)(2,1)} fusion(f32[3,1024,1024]{1,2,0:T(8,128)S(1)} %get-tuple-element.190, f32[3,1024,1024]{1,2,0:T(8,128)S(1)} %bitcast.261, f32[3,1024]{1,0:T(4,128)S(1)} %get-tuple-element.189, f32[3,1024]{1,0:T(4,128)S(1)} %copy-done.39), kind=kLoop, calls=%fused_computation | loop fusion | flops 12582912 | bytes 31481856 | tf_op jit(solution)/shard_map/convert_element_type | solution.py:66
  204.0 5.0 %fusion.51 = bf16[3,64,1024]{2,1,0:T(8,128)(2,1)S(1)} fusion(bf16[1024,3,64]{0,2,1:T(8,128)(2,1)S(1)} %bitcast.288, bf16[3,1024,1024]{1,2,0:T(8,128)(2,1)} %multiply_convert_fusion), kind=kOutput, calls=%fused_computation.173 | convolution fusion | flops 403046400 | bytes 7077888 | tf_op jit(solution)/shard_map/hqk,qhd->khd/dot_general | solution.py:68
  215.7 4.3 %multiply_reduce_fusion.19 = (f32[192]{0:T(256)}, bf16[1024,192]{0,1:T(8,128)(2,1)}) fusion(f32[1024,192]{0,1:T(8,128)} %bitcast.308, f32[192]{0:T(256)} %copy-done.77, bf16[192,768]{1,0:T(8,128)(2,1)} %param.29, bf16[512,768]{1,0:T(8,128)(2,1)} %copy-done.84, bf16[512,768]{1,0:T(8,128)(2,1)} %copy-done.44, pred[]{:T(512)S(6)} %eq.52), kind=kOutput, calls=%fused_computation.220 | convolution fusion | flops 309854016 | bytes 3048961 | tf_op jit(solution)/shard_map/dot_general | solution.py:38
  221.8 7.7 %multiply_reduce_fusion.1 = (f32[3,1024]{1,0:T(4,128)S(1)}, f32[3,1024,1024]{1,2,0:T(8,128)S(1)}) fusion(f32[3,1024,1024]{1,2,0:T(8,128)} %copy-done.2, f32[3,1024]{1,0:T(4,128)} %log_add_fusion.1, bf16[1024,3,64]{0,2,1:T(8,128)(2,1)} %bitcast.289, bf16[1024,3,64]{0,2,1:T(8,128)(2,1)} %bitcast.294), kind=kOutput, calls=%fused_computation.4 | convolution fusion | flops 412087296 | bytes 25976832 | tf_op jit(solution)/shard_map/qhd,khd->hqk/dot_general | solution.py:64
  230.2 5.6 %multiply_convert_fusion.1 = bf16[3,1024,1024]{1,2,0:T(8,128)(2,1)} fusion(f32[3,1024,1024]{1,2,0:T(8,128)S(1)} %get-tuple-element.188, f32[3,1024,1024]{1,2,0:T(8,128)S(1)} %bitcast.259, f32[3,1024]{1,0:T(4,128)S(1)} %get-tuple-element.187, f32[3,1024]{1,0:T(4,128)S(1)} %copy-done.38), kind=kLoop, calls=%fused_computation.3 | loop fusion | flops 12582912 | bytes 31481856 | tf_op jit(solution)/shard_map/convert_element_type | solution.py:66
  235.9 5.1 %fusion.49 = bf16[3,64,1024]{2,1,0:T(8,128)(2,1)S(1)} fusion(bf16[1024,3,64]{0,2,1:T(8,128)(2,1)} %bitcast.286, bf16[3,1024,1024]{1,2,0:T(8,128)(2,1)} %multiply_convert_fusion.1), kind=kOutput, calls=%fused_computation.171 | convolution fusion | flops 403046400 | bytes 7077888 | tf_op jit(solution)/shard_map/hqk,qhd->khd/dot_general | solution.py:68
  245.1 3.2 convert_element_type.289
  265.9 4.4 %convolution_add_fusion = f32[1024,768]{1,0:T(8,128)} fusion(f32[1024,768]{1,0:T(8,128)S(1)} %fusion.85, bf16[768,768]{1,0:T(8,128)(2,1)} %collective-permute-done, bf16[1024,192]{0,1:T(8,128)(2,1)S(1)} %bitcast.274, bf16[1024,192]{0,1:T(8,128)(2,1)S(1)} %bitcast.277, bf16[1024,192]{0,1:T(8,128)(2,1)S(1)} %bitcast.280), kind=kOutput, calls=%fused_computation.49 | convolution fusion | flops 910295040 | bytes 8355840 | tf_op jit(solution)/shard_map/dot_general | solution.py:38
  270.4 38.1 %collective-permute-done.14 = f32[20,768]{1,0:T(8,128)S(1)} collective-permute-done((f32[20,768]{1,0:T(8,128)S(1)}, f32[20,768]{1,0:T(8,128)S(1)}, u32[]{:S(2)}, u32[]{:S(2)}) %collective-permute-start.14) | collective-permute-done | bytes 61472 | tf_op jit(solution)/shard_map/ppermute | solution.py:34
  330.8 6.9 %fusion.15 = f32[768,1536]{0,1:T(8,128)} fusion(f32[2,768,1536]{1,2,0:T(8,128)} %copy-done.6, f32[768,768]{0,1:T(8,128)S(1)} %fusion.127, f32[768,768]{0,1:T(8,128)} %fusion.126, bf16[768,1536]{0,1:T(8,128)(2,1)} %collective-permute-done.19), kind=kLoop, calls=%fused_computation.27 | loop fusion | flops 4718592 | bytes 16515072 | tf_op jit(solution)/shard_map/add | solution.py:171
  337.7 6.3 %copy.94 = f32[768,1536]{1,0:T(8,128)} copy(f32[768,1536]{0,1:T(8,128)} %fusion.15) | data formatting | bytes 9437184 | tf_op jit(solution)/shard_map/add | solution.py:171
  352.7 18.3 %collective-permute-done.20 = bf16[4,96,1536]{2,1,0:T(8,128)(2,1)S(1)} collective-permute-done((bf16[4,96,1536]{2,1,0:T(8,128)(2,1)S(1)}, bf16[4,96,1536]{2,1,0:T(8,128)(2,1)S(1)}, u32[]{:S(2)}, u32[]{:S(2)}) %collective-permute-start.20) | collective-permute-done | bytes 1179680 | tf_op jit(solution)/shard_map/ppermute | solution.py:34
  375.4 10.4 %collective-permute-done.21 = bf16[2,96,1536]{2,1,0:T(8,128)(2,1)S(1)} collective-permute-done((bf16[2,96,1536]{2,1,0:T(8,128)(2,1)S(1)}, bf16[2,96,1536]{2,1,0:T(8,128)(2,1)S(1)}, u32[]{:S(2)}, u32[]{:S(2)}) %collective-permute-start.21) | collective-permute-done | bytes 589856 | tf_op jit(solution)/shard_map/ppermute | solution.py:34
  389.7 8.5 %collective-permute-done.22 = bf16[1,96,1536]{2,1,0:T(8,128)(2,1)S(1)} collective-permute-done((bf16[1,96,1536]{2,1,0:T(8,128)(2,1)S(1)}, bf16[1,96,1536]{2,1,0:T(8,128)(2,1)S(1)}, u32[]{:S(2)}, u32[]{:S(2)}) %collective-permute-start.22) | collective-permute-done | bytes 294944 | tf_op jit(solution)/shard_map/ppermute | solution.py:34
  (393 shorter events, 183.9 us)
Async XLA Ops:
  4.9 28.6 %collective-permute-start.1 = (f32[3,768]{1,0:T(4,128)S(1)}, f32[3,768]{1,0:T(4,128)S(1)}, u32[]{:S(2)}, u32[]{:S(2)}) collective-permute-start(f32[3,768]{1,0:T(4,128)S(1)} %get-tuple-element.166), channel_id=1, source_target_pairs={{0,2},{1,3},{2,0},{3,1},{4,6},{5,7},{6,4},{7,5},{8,10},{9,11},{10,... | collective-permute-start | bytes 27656 | tf_op jit(solution)/shard_map/ppermute | solution.py:34
  9.2 29.1 %collective-permute-start = (bf16[768,768]{1,0:T(8,128)(2,1)S(1)}, bf16[768,768]{1,0:T(8,128)(2,1)}, u32[]{:S(2)}, u32[]{:S(2)}) collective-permute-start(bf16[768,768]{1,0:T(8,128)(2,1)S(1)} %pad_maximum_fusion.2), channel_id=1, source_target_pairs={{0,2},{1,3},{2,0},{3,1},{4,6},{5,7},{6,4},{7,5},{8,10},{9,11},{10,... | collective-permute-start | bytes 3538952 | tf_op jit(solution)/shard_map/ppermute | solution.py:34
  10.9 76.4 %collective-permute-start.5 = (bf16[2,768,768]{2,1,0:T(8,128)(2,1)}, bf16[2,768,768]{2,1,0:T(8,128)(2,1)}, u32[]{:S(2)}, u32[]{:S(2)}) collective-permute-start(bf16[2,768,768]{2,1,0:T(8,128)(2,1)} %pad_maximum_fusion.1), channel_id=1, source_target_pairs={{0,2},{1,3},{2,0},{3,1},{4,6},{5,7},{6,4},{7,5},{8,10},{9,11},{10,... | collective-permute-start | bytes 7077896 | tf_op jit(solution)/shard_map/ppermute | solution.py:34
  55.9 31.4 %collective-permute-start.2 = (f32[512,768]{1,0:T(8,128)}, f32[512,768]{1,0:T(8,128)}, u32[]{:S(2)}, u32[]{:S(2)}) collective-permute-start(f32[512,768]{1,0:T(8,128)} %constant_dynamic-slice_fusion.4), channel_id=1, source_target_pairs={{0,1},{1,0},{2,3},{3,2},{4,5},{5,4},{6,7},{7,6},{8,9},{9,8},{10,11... | collective-permute-start | bytes 4718600 | tf_op jit(solution)/shard_map/ppermute | solution.py:34
  55.9 59.6 %collective-permute-start.3 = (bf16[2,768,768]{2,1,0:T(8,128)(2,1)}, bf16[2,768,768]{2,1,0:T(8,128)(2,1)}, u32[]{:S(2)}, u32[]{:S(2)}) collective-permute-start(bf16[2,768,768]{2,1,0:T(8,128)(2,1)} %pad_maximum_fusion.1), channel_id=1, source_target_pairs={{0,1},{1,0},{2,3},{3,2},{4,5},{5,4},{6,7},{7,6},{8,9},{9,8},{10,11... | collective-permute-start | bytes 7077896 | tf_op jit(solution)/shard_map/ppermute | solution.py:34
  59.6 3.1 collective-permute-start.4
  87.3 41.1 %collective-permute-start.6 = (bf16[2,768,768]{2,1,0:T(8,128)(2,1)}, bf16[2,768,768]{2,1,0:T(8,128)(2,1)S(1)}, u32[]{:S(2)}, u32[]{:S(2)}) collective-permute-start(bf16[2,768,768]{2,1,0:T(8,128)(2,1)} %collective-permute-done.5), channel_id=1, source_target_pairs={{0,1},{1,0},{2,3},{3,2},{4,5},{5,4},{6,7},{7,6},{8,9},{9,8},{10,11... | collective-permute-start | bytes 7077896 | tf_op jit(solution)/shard_map/ppermute | solution.py:34
  172.2 17.7 %collective-permute-start.7 = (bf16[512,768]{1,0:T(8,128)(2,1)S(1)}, bf16[512,768]{1,0:T(8,128)(2,1)S(1)}, u32[]{:S(2)}, u32[]{:S(2)}) collective-permute-start(bf16[512,768]{1,0:T(8,128)(2,1)S(1)} %get-tuple-element.150), channel_id=1, source_target_pairs={{0,1},{1,0},{2,3},{3,2},{4,5},{5,4},{6,7},{7,6},{8,9},{9,8},{10,11... | collective-permute-start | bytes 2359304 | tf_op jit(solution)/shard_map/ppermute | solution.py:34
  185.4 59.7 %collective-permute-start.18 = (bf16[2,768,1536]{1,2,0:T(8,128)(2,1)}, bf16[2,768,1536]{1,2,0:T(8,128)(2,1)}, u32[]{:S(2)}, u32[]{:S(2)}) collective-permute-start(bf16[2,768,1536]{1,2,0:T(8,128)(2,1)} %pad_maximum_fusion), channel_id=1, source_target_pairs={{0,1},{1,0},{2,3},{3,2},{4,5},{5,4},{6,7},{7,6},{8,9},{9,8},{10,11... | collective-permute-start | bytes 14155784 | tf_op jit(solution)/shard_map/ppermute | solution.py:34
  214.1 106.6 %collective-permute-start.9 = (bf16[768,768]{0,1:T(8,128)(2,1)}, bf16[768,768]{0,1:T(8,128)(2,1)}, u32[]{:S(2)}, u32[]{:S(2)}) collective-permute-start(bf16[768,768]{0,1:T(8,128)(2,1)} %pad_maximum_fusion.5), channel_id=1, source_target_pairs={{0,2},{1,3},{2,0},{3,1},{4,6},{5,7},{6,4},{7,5},{8,10},{9,11},{10,... | collective-permute-start | bytes 3538952 | tf_op jit(solution)/shard_map/ppermute | solution.py:34
  253.3 77.6 %collective-permute-start.19 = (bf16[768,1536]{0,1:T(8,128)(2,1)}, bf16[768,1536]{0,1:T(8,128)(2,1)}, u32[]{:S(2)}, u32[]{:S(2)}) collective-permute-start(bf16[768,1536]{0,1:T(8,128)(2,1)} %fusion.13), channel_id=1, source_target_pairs={{0,2},{1,3},{2,0},{3,1},{4,6},{5,7},{6,4},{7,5},{8,10},{9,11},{10,... | collective-permute-start | bytes 7077896 | tf_op jit(solution)/shard_map/ppermute | solution.py:34
  262.5 3.0 collective-permute-start.13
  265.6 44.8 %copy-start.26 = (bf16[1024,192]{0,1:T(8,128)(2,1)S(1)}, bf16[1024,192]{0,1:T(8,128)(2,1)}, u32[]{:S(2)}) copy-start(bf16[1024,192]{0,1:T(8,128)(2,1)} %copy-done.25) | copy-start | bytes 1179652
  265.6 42.9 %collective-permute-start.14 = (f32[20,768]{1,0:T(8,128)S(1)}, f32[20,768]{1,0:T(8,128)S(1)}, u32[]{:S(2)}, u32[]{:S(2)}) collective-permute-start(f32[20,768]{1,0:T(8,128)S(1)} %add.371), channel_id=1, source_target_pairs={{0,2},{1,3},{2,0},{3,1},{4,6},{5,7},{6,4},{7,5},{8,10},{9,11},{10,... | collective-permute-start | bytes 184328 | tf_op jit(solution)/shard_map/ppermute | solution.py:34
  308.6 4.4 %collective-permute-start.15 = (f32[20,768]{1,0:T(8,128)S(1)}, f32[20,768]{1,0:T(8,128)S(1)}, u32[]{:S(2)}, u32[]{:S(2)}) collective-permute-start(f32[20,768]{1,0:T(8,128)S(1)} %add.372), channel_id=1, source_target_pairs={{0,4},{4,0},{8,12},{12,8},{16,20},{20,16},{24,28},{28,24},{1,5},{5... | collective-permute-start | bytes 184328 | tf_op jit(solution)/shard_map/ppermute | solution.py:34
  313.0 4.4 %collective-permute-start.16 = (f32[20,768]{1,0:T(8,128)S(1)}, f32[20,768]{1,0:T(8,128)S(1)}, u32[]{:S(2)}, u32[]{:S(2)}) collective-permute-start(f32[20,768]{1,0:T(8,128)S(1)} %add.373), channel_id=1, source_target_pairs={{0,8},{4,12},{8,0},{12,4},{16,24},{20,28},{24,16},{28,20},{1,9},{5... | collective-permute-start | bytes 184328 | tf_op jit(solution)/shard_map/ppermute | solution.py:34
  317.4 30.2 %collective-permute-start.17 = (f32[20,768]{1,0:T(8,128)S(1)}, f32[20,768]{1,0:T(8,128)S(1)}, u32[]{:S(2)}, u32[]{:S(2)}) collective-permute-start(f32[20,768]{1,0:T(8,128)S(1)} %add.374), channel_id=1, source_target_pairs={{0,16},{4,20},{8,24},{12,28},{16,0},{20,4},{24,8},{28,12},{1,17},{... | collective-permute-start | bytes 184328 | tf_op jit(solution)/shard_map/ppermute | solution.py:34
  329.3 20.7 %collective-permute-start.10 = (bf16[4,96,768]{2,1,0:T(8,128)(2,1)}, bf16[4,96,768]{2,1,0:T(8,128)(2,1)}, u32[]{:S(2)}, u32[]{:S(2)}) collective-permute-start(bf16[4,96,768]{2,1,0:T(8,128)(2,1)} %fusion.81), channel_id=1, source_target_pairs={{0,4},{4,0},{8,12},{12,8},{16,20},{20,16},{24,28},{28,24},{1,5},{5... | collective-permute-start | bytes 1769480 | tf_op jit(solution)/shard_map/ppermute | solution.py:34
  346.8 24.2 %collective-permute-start.20 = (bf16[4,96,1536]{2,1,0:T(8,128)(2,1)S(1)}, bf16[4,96,1536]{2,1,0:T(8,128)(2,1)S(1)}, u32[]{:S(2)}, u32[]{:S(2)}) collective-permute-start(bf16[4,96,1536]{2,1,0:T(8,128)(2,1)S(1)} %fusion.58), channel_id=1, source_target_pairs={{0,4},{4,0},{8,12},{12,8},{16,20},{20,16},{24,28},{28,24},{1,5},{5... | collective-permute-start | bytes 3538952 | tf_op jit(solution)/shard_map/ppermute | solution.py:34
  347.5 25.8 %collective-permute-start.8 = (f32[512,768]{1,0:T(8,128)S(1)}, f32[512,768]{1,0:T(8,128)S(1)}, u32[]{:S(2)}, u32[]{:S(2)}) collective-permute-start(f32[512,768]{1,0:T(8,128)S(1)} %constant_dynamic-slice_fusion.3), channel_id=1, source_target_pairs={{0,1},{1,0},{2,3},{3,2},{4,5},{5,4},{6,7},{7,6},{8,9},{9,8},{10,11... | collective-permute-start | bytes 4718600 | tf_op jit(solution)/shard_map/ppermute | solution.py:34
  351.4 23.5 %collective-permute-start.11 = (bf16[2,96,768]{2,1,0:T(8,128)(2,1)S(1)}, bf16[2,96,768]{2,1,0:T(8,128)(2,1)S(1)}, u32[]{:S(2)}, u32[]{:S(2)}) collective-permute-start(bf16[2,96,768]{2,1,0:T(8,128)(2,1)S(1)} %fusion.86), channel_id=1, source_target_pairs={{0,8},{4,12},{8,0},{12,4},{16,24},{20,28},{24,16},{28,20},{1,9},{5... | collective-permute-start | bytes 884744 | tf_op jit(solution)/shard_map/ppermute | solution.py:34
  371.7 14.1 %collective-permute-start.21 = (bf16[2,96,1536]{2,1,0:T(8,128)(2,1)S(1)}, bf16[2,96,1536]{2,1,0:T(8,128)(2,1)S(1)}, u32[]{:S(2)}, u32[]{:S(2)}) collective-permute-start(bf16[2,96,1536]{2,1,0:T(8,128)(2,1)S(1)} %fusion.82), channel_id=1, source_target_pairs={{0,8},{4,12},{8,0},{12,4},{16,24},{20,28},{24,16},{28,20},{1,9},{5... | collective-permute-start | bytes 1769480 | tf_op jit(solution)/shard_map/ppermute | solution.py:34
  375.0 13.2 %collective-permute-start.12 = (bf16[1,96,768]{2,1,0:T(8,128)(2,1)S(1)}, bf16[1,96,768]{2,1,0:T(8,128)(2,1)S(1)}, u32[]{:S(2)}, u32[]{:S(2)}) collective-permute-start(bf16[1,96,768]{2,1,0:T(8,128)(2,1)S(1)} %select_convert_fusion.5), channel_id=1, source_target_pairs={{0,16},{4,20},{8,24},{12,28},{16,0},{20,4},{24,8},{28,12},{1,17},{... | collective-permute-start | bytes 442376 | tf_op jit(solution)/shard_map/ppermute | solution.py:34
  386.1 12.1 %collective-permute-start.22 = (bf16[1,96,1536]{2,1,0:T(8,128)(2,1)S(1)}, bf16[1,96,1536]{2,1,0:T(8,128)(2,1)S(1)}, u32[]{:S(2)}, u32[]{:S(2)}) collective-permute-start(bf16[1,96,1536]{2,1,0:T(8,128)(2,1)S(1)} %select_convert_fusion.3), channel_id=1, source_target_pairs={{0,16},{4,20},{8,24},{12,28},{16,0},{20,4},{24,8},{28,12},{1,17},{... | collective-permute-start | bytes 884744 | tf_op jit(solution)/shard_map/ppermute | solution.py:34
  (94 other events, 688.7 us)
